TPU v7x, 32 devices: a whole 2x2x4 slice. The times are simulated.
32 devices in a mesh: pair: 4 (over x, core), row: 2 (over y), col: 4 (over z).
Axes of the slice: x: 2, y: 2, z: 4, core: 2. Of those that a mesh axis runs over, the one named last changes fastest.
Arguments:
- coords: float32 [4, 30, 512], P('pair', None, ('row', 'col')), may hold values from -1.6 to 1.6
- final_coords: float32 [30, 512], P(None, ('row', 'col')), may hold values from -1.6 to 1.6
- growth: float32 [4, 512], P('pair', ('row', 'col')), may hold values from 0.4 to 2.5
- counts: int32 [5], replicated, may hold values from 256 to 512, as said below
- labels: int32 [512], P(('row', 'col')), may hold values from 0 to 15
Outputs:
- fates: float32 [4, 16, 512], P('pair', None, ('row', 'col'))
- mass: float32 [4, 512], P('pair', ('row', 'col'))
Inputs may be any that keep to these rules, and one draw needn't show every extreme that they name: The cells of a timepoint are its first counts positions; some timepoint has all 512.
All inputs are finite; a program needn't handle non-finite values.
Results may differ from a plain program's by a relative error of at most 0.0001.
Values sent between devices are 32-bit elements; how exact they have to be, the bound alone decides.
A program may use at most 64 MiB of HBM per device.

v0:
```python
import functools
import jax
import jax.numpy as jnp
from jax import lax
from jax.experimental import pallas as pl
from jax.experimental.pallas import tpu as pltpu
from jax.sharding import PartitionSpec as P

CLASSES = 16
FUSED_BYTES = 16 * 1024 * 1024


cost_scale = 1.0
source_power = 0.5
target_power = 50.0 / 51.0


def shifted_2(block, axis, distance):
    devices = range(lax.axis_size(axis))
    route = [(i - distance, i) for i in devices if i - distance in devices]
    return lax.ppermute(block, axis, route)


def kernel_tile(sources, targets):
    cross = lax.dot_general(
        sources,
        targets,
        (((0,), (0,)), ((), ())),
        precision=lax.Precision.HIGHEST,
        preferred_element_type=jnp.float32,
    )
    source_norms = jnp.sum(sources * sources, axis=0)
    target_norms = jnp.sum(targets * targets, axis=0)
    return jnp.exp(-(source_norms[:, None] + target_norms[None, :] - 2.0 * cross) / cost_scale)


def forward(kernel, weights):
    return lax.dot_general(
        weights,
        kernel,
        (((1,), (1,)), ((), ())),
        precision=lax.Precision.HIGHEST,
        preferred_element_type=jnp.float32,
    )


def backward(kernel, scales):
    return jnp.dot(
        scales, kernel, precision=lax.Precision.HIGHEST, preferred_element_type=jnp.float32
    )


def per_device(coords, final_coords, growth, counts, labels):
    tile = coords.shape[2]
    n_pair = lax.axis_size("pair")
    n_row = lax.axis_size("row")
    n_col = lax.axis_size("col")
    pair_at = lax.axis_index("pair")
    row_at = lax.axis_index("row")
    col_at = lax.axis_index("col")
    source_count = n_col * tile
    target_count = n_row * tile
    own_coords = coords[0]
    sources, source_growth = (
        lax.all_gather(own_coords, "col", axis=1, tiled=True),
        lax.all_gather(growth[0], "col", axis=0, tiled=True),
    )
    shifted = shifted_2(own_coords, "pair", -1)
    is_last = pair_at == n_pair - 1
    own_targets = jnp.where(is_last, final_coords, shifted)
    label_values = labels.astype(jnp.float32)
    position = lax.iota(jnp.int32, target_count)
    targets, target_labels = (
        lax.all_gather(own_targets, "row", axis=1, tiled=True),
        lax.all_gather(label_values, "row", axis=0, tiled=True),
    )
    target_index = position // tile * (n_col * tile) + col_at * tile + position % tile

    def hand_over(fates_now):
        incoming = shifted_2(fates_now, "pair", -1)
        return lax.all_gather(incoming, "row", axis=1, tiled=True)

    source_number = counts[pair_at]
    target_number = counts[pair_at + 1]
    source_total = source_number.astype(jnp.float32)
    target_total = target_number.astype(jnp.float32)
    source_index = row_at * source_count + lax.iota(jnp.int32, source_count)
    source_valid = source_index < source_number
    target_valid = target_index < target_number
    kernel = kernel_tile(sources, targets)
    start_terms = forward(kernel, target_valid.astype(jnp.float32)[None, :])[0]
    start_rows = lax.psum(start_terms, "col")
    source_mass = jnp.where(source_valid, source_growth / source_total, 0.0)
    scale_u = jnp.where(source_valid, jnp.power(source_mass / start_rows, source_power), 0.0)
    column_terms = backward(kernel, scale_u)
    column_totals = lax.psum(column_terms, "row")
    target_mass = target_valid.astype(jnp.float32) / target_total
    scale_v = jnp.where(target_valid, jnp.power(target_mass / column_totals, target_power), 0.0)
    own_offset = col_at * tile
    own_valid = lax.dynamic_slice_in_dim(source_valid, own_offset, tile, 0)
    own_scale = lax.dynamic_slice_in_dim(scale_u, own_offset, tile, 0)
    class_values = lax.iota(jnp.int32, CLASSES).astype(jnp.float32)
    label_table = jnp.where(
        (target_labels[None, :] == class_values[:, None]) & target_valid[None, :], 1.0, 0.0
    ).astype(jnp.float32)
    empty = jnp.zeros((CLASSES, tile), jnp.float32)
    final_terms = forward(kernel, scale_v[None, :])[0]
    final_rows = lax.psum(final_terms, "col")
    own_rows = lax.dynamic_slice_in_dim(final_rows, own_offset, tile, 0)
    safe_rows = jnp.where(own_valid, own_rows, 1.0)

    def advance(turn, fates_now):
        carried = jnp.where(is_last, label_table, hand_over(fates_now))
        terms = forward(kernel, carried * scale_v[None, :])
        sums = lax.psum_scatter(terms, "col", scatter_dimension=1, tiled=True)
        return jnp.where(own_valid[None, :], sums / safe_rows[None, :], 0.0)

    fates = lax.fori_loop(0, n_pair, advance, empty)
    mass = jnp.where(own_valid, source_total * own_scale * own_rows, 0.0)
    return (fates[None], mass[None])


LANES = 128
HALF = 16
BIG = 1e30
MESH = pl.DeviceIdType.MESH


def split3(a):
    first = a.astype(jnp.bfloat16)
    rest = a - first.astype(jnp.float32)
    second = rest.astype(jnp.bfloat16)
    third = (rest - second.astype(jnp.float32)).astype(jnp.bfloat16)
    return first, second, third


def split2(a):
    first = a.astype(jnp.bfloat16)
    return first, (a - first.astype(jnp.float32)).astype(jnp.bfloat16)


def dot(a, b, dims):
    return lax.dot_general(a, b, (dims, ((), ())), preferred_element_type=jnp.float32)


def packed(block, extra):
    low = block[:HALF]
    rest = block.shape[0] - HALF
    fill = jnp.zeros((HALF - rest - 1, block.shape[1]), jnp.float32)
    high = jnp.concatenate([block[HALF:], extra, fill], axis=0)
    return jnp.concatenate([low, high], axis=1)


def unpacked(ref):
    lows, highs = [], []
    lane = lax.broadcasted_iota(jnp.int32, (HALF, LANES), 1)
    for j in range(ref.shape[0] // 2):
        a, b = ref[2 * j], ref[2 * j + 1]
        swap_a, swap_b = pltpu.roll(a, LANES // 2, 1), pltpu.roll(b, LANES // 2, 1)
        lows.append(jnp.where(lane < LANES // 2, a, swap_b))
        highs.append(jnp.where(lane < LANES // 2, swap_a, b))
    low, high = jnp.concatenate(lows, axis=1), jnp.concatenate(highs, axis=1)
    return jnp.concatenate([low, high], axis=0)


def own_part(ref, value, mine, tile):
    for j in range(ref.shape[0]):
        ref[j] = value[:, j * LANES : (j + 1) * LANES]
    chunk = ref[mine // 2]
    return pltpu.roll(chunk, (mine % 2) * tile, 1)[:, :tile]


def fused(
    sizes,
    counts_ref,
    coords_in,
    final_in,
    growth_in,
    labels_in,
    fates_ref,
    mass_ref,
    coords_ref,
    final_ref,
    growth_ref,
    labels_ref,
    in_sems,
    xg,
    yg,
    k1,
    k2,
    fin,
    fout,
    pick_f,
    pick_m,
    x_send,
    x_recv,
    y_send,
    y_recv,
    z_send,
    f_send,
    f_recv,
):
    n_pair, n_row, n_col, tile = sizes
    n_block = n_row * n_col
    cells = n_block * tile
    pca = coords_ref.shape[0]
    last = n_pair - 1
    pair_at = lax.axis_index("pair")
    row_at = lax.axis_index("row")
    col_at = lax.axis_index("col")
    mine = row_at * n_col + col_at
    is_last = pair_at == last
    not_last = pair_at < last
    not_first = pair_at > 0

    def others(act):
        for block in range(n_block):
            pl.when(mine != block)(functools.partial(act, block))

    barrier = pltpu.get_barrier_semaphore()

    @others
    def _(block):
        r, c = divmod(block, n_col)
        pl.semaphore_signal(barrier, inc=1, device_id=(pair_at, r, c), device_id_type=MESH)

    @pl.when(not_last)
    def _():
        pl.semaphore_signal(
            barrier, inc=1, device_id=(pair_at + 1, row_at, col_at), device_id_type=MESH
        )

    source_loads = (
        pltpu.make_async_copy(coords_in, coords_ref, in_sems.at[0]),
        pltpu.make_async_copy(growth_in, growth_ref, in_sems.at[1]),
    )
    target_loads = (
        pltpu.make_async_copy(final_in, final_ref, in_sems.at[2]),
        pltpu.make_async_copy(labels_in, labels_ref, in_sems.at[3]),
    )
    for load in source_loads + target_loads:
        load.start()
    for load in source_loads + target_loads:
        load.wait()
    xg[mine] = packed(coords_ref[:, 0, :], growth_ref[...])

    @pl.when(is_last)
    def _():
        yg[mine] = packed(final_ref[...], labels_ref[...].astype(jnp.float32))

    @pl.when(not_first)
    def _():
        pl.semaphore_wait(barrier, n_block)

    @pl.when(pair_at == 0)
    def _():
        pl.semaphore_wait(barrier, n_block - 1)

    def x_copy(block):
        r, c = divmod(block, n_col)
        return pltpu.make_async_remote_copy(
            src_ref=xg.at[mine],
            dst_ref=xg.at[mine],
            send_sem=x_send.at[block],
            recv_sem=x_recv.at[mine],
            device_id=(pair_at, r, c),
            device_id_type=MESH,
        )

    def final_copy(block):
        r, c = divmod(block, n_col)
        return pltpu.make_async_remote_copy(
            src_ref=yg.at[mine],
            dst_ref=yg.at[mine],
            send_sem=z_send.at[block],
            recv_sem=y_recv.at[mine],
            device_id=(pair_at, r, c),
            device_id_type=MESH,
        )

    def relay(block):
        return pltpu.make_async_remote_copy(
            src_ref=xg.at[block],
            dst_ref=yg.at[block],
            send_sem=y_send.at[block],
            recv_sem=y_recv.at[block],
            device_id=(jnp.maximum(pair_at - 1, 0), row_at, col_at),
            device_id_type=MESH,
        )

    def arrival(buffer, sems, other):
        return pltpu.make_async_remote_copy(
            src_ref=buffer.at[other],
            dst_ref=buffer.at[other],
            send_sem=x_send.at[0],
            recv_sem=sems.at[other],
            device_id=(pair_at, row_at, col_at),
            device_id_type=MESH,
        )

    @others
    def _(block):
        x_copy(block).start()

        @pl.when(is_last)
        def _():
            final_copy(block).start()

    for block in range(n_block):

        @pl.when(mine != block)
        def _(block=block):
            arrival(xg, x_recv, block).wait_recv()

        @pl.when(not_first)
        def _(block=block):
            relay(block).start()

    for block in range(n_block):

        @pl.when(not_last | (mine != block))
        def _(block=block):
            arrival(yg, y_recv, block).wait_recv()

    source_number = counts_ref[pair_at]
    target_number = counts_ref[pair_at + 1]
    source_total = source_number.astype(jnp.float32)
    target_total = target_number.astype(jnp.float32)
    index = lax.broadcasted_iota(jnp.int32, (1, cells), 1)
    source_valid = index < source_number
    target_valid = index < target_number

    x = unpacked(xg)
    y = unpacked(yg)
    growth = x[pca : pca + 1]
    labels = y[pca : pca + 1]
    feature = lax.broadcasted_iota(jnp.int32, x.shape, 0)
    x = jnp.where(feature < pca, x, 0.0)
    y = jnp.where(feature < pca, y, 0.0)
    x_norm = jnp.sum(x * x, axis=0, keepdims=True)
    y_norm = jnp.where(target_valid, jnp.sum(y * y, axis=0, keepdims=True), BIG)
    a = jnp.where(feature < pca, x + x, jnp.where(feature == pca, -x_norm, 1.0))
    b = jnp.where(feature < pca, y, jnp.where(feature == pca, 1.0, -y_norm))
    a1, a2, a3 = split3(a)
    b1, b2, b3 = split3(b)
    left = jnp.concatenate([b1, b1, b2, b2, b1, b3], axis=0)
    right = jnp.concatenate([a1, a2, a1, a2, a3, a1], axis=0)
    totals = jnp.zeros((1, cells), jnp.float32)
    for j in range(cells // LANES):
        rows = slice(j * LANES, (j + 1) * LANES)
        values = jnp.exp(dot(left[:, rows], right, ((0,), (0,))))
        totals = totals + jnp.sum(values, axis=0, keepdims=True)
        high, low = split2(values)
        k1[rows, :] = high
        k2[rows, :] = low
    scale_u = jnp.where(source_valid, jnp.sqrt(growth / source_total / totals), 0.0)
    u1, u2 = split2(jnp.broadcast_to(scale_u, (HALF, cells)))
    u12 = jnp.concatenate([u1, u2], axis=0)
    column = dot(u12, k1[...], ((1,), (1,)))
    column_low = dot(u1, k2[...], ((1,), (1,)))
    column = column[:1] + column[HALF : HALF + 1] + column_low[:1]
    ratio = 1.0 / target_total / jnp.where(target_valid, column, 1.0)
    scale_v = jnp.where(target_valid, jnp.exp(target_power * jnp.log(ratio)), 0.0)

    def transported(weights):
        w1, w2 = split2(weights)
        both = dot(jnp.concatenate([w1, w2], axis=0), k1[...], ((1,), (0,)))
        return both[:CLASSES] + both[CLASSES:] + dot(w1, k2[...], ((1,), (0,)))

    row_totals = transported(jnp.broadcast_to(scale_v, (CLASSES, cells)))[:1]
    mass = jnp.where(source_valid, source_total * scale_u * row_totals, 0.0)
    mass_ref[...] = own_part(pick_m, jnp.broadcast_to(mass, (8, cells)), mine, tile)[:1]
    share = jnp.where(source_valid, 1.0 / row_totals, 0.0)

    f_copy = pltpu.make_async_remote_copy(
        src_ref=fout,
        dst_ref=fin,
        send_sem=f_send,
        recv_sem=f_recv,
        device_id=(jnp.maximum(pair_at - 1, 0), row_at, col_at),
        device_id_type=MESH,
    )

    @pl.when(is_last)
    def _():
        class_values = lax.broadcasted_iota(jnp.int32, (CLASSES, cells), 0).astype(jnp.float32)
        fin[...] = jnp.where((labels == class_values) & target_valid, 1.0, 0.0)

    @pl.when(not_last)
    def _():
        f_copy.wait_recv()

    fates = transported(fin[...] * scale_v) * share
    fout[...] = fates

    @pl.when(not_first)
    def _():
        f_copy.start()

    fates_ref[0] = own_part(pick_f, fates, mine, tile)

    @others
    def _(block):
        x_copy(block).wait_send()

    @pl.when(not_first)
    def _():
        for block in range(n_block):
            relay(block).wait_send()
        f_copy.wait_send()

    @pl.when(is_last)
    def _():
        @others
        def _(block):
            final_copy(block).wait_send()


def per_device_fused(coords, final_coords, growth, counts, labels):
    tile = coords.shape[2]
    n_pair = lax.axis_size("pair")
    n_row = lax.axis_size("row")
    n_col = lax.axis_size("col")
    n_block = n_row * n_col
    cells = n_block * tile
    vmem = pl.BlockSpec(memory_space=pltpu.VMEM)
    dma = pltpu.SemaphoreType.DMA
    return pl.pallas_call(
        functools.partial(fused, (n_pair, n_row, n_col, tile)),
        out_shape=(
            pltpu.VMEM((1, CLASSES, tile), jnp.float32),
            pltpu.VMEM((1, tile), jnp.float32),
        ),
        in_specs=[pl.BlockSpec(memory_space=pltpu.SMEM)] + [pl.BlockSpec(memory_space=pl.ANY)] * 4,
        out_specs=(vmem, vmem),
        scratch_shapes=[
            pltpu.VMEM((coords.shape[1], 1, tile), jnp.float32),
            pltpu.VMEM((coords.shape[1], tile), jnp.float32),
            pltpu.VMEM((1, tile), jnp.float32),
            pltpu.VMEM((1, tile), jnp.int32),
            dma((4,)),
            pltpu.VMEM((n_block, HALF, LANES), jnp.float32),
            pltpu.VMEM((n_block, HALF, LANES), jnp.float32),
            pltpu.VMEM((cells, cells), jnp.bfloat16),
            pltpu.VMEM((cells, cells), jnp.bfloat16),
            pltpu.VMEM((CLASSES, cells), jnp.float32),
            pltpu.VMEM((CLASSES, cells), jnp.float32),
            pltpu.VMEM((cells // LANES, CLASSES, LANES), jnp.float32),
            pltpu.VMEM((cells // LANES, 8, LANES), jnp.float32),
            dma((n_block,)),
            dma((n_block,)),
            dma((n_block,)),
            dma((n_block,)),
            dma((n_block,)),
            dma,
            dma,
        ],
        compiler_params=pltpu.CompilerParams(collective_id=0, has_side_effects=True),
    )(counts, jnp.transpose(coords, (1, 0, 2)), final_coords, growth, labels[None, :])


def solution(mesh):
    placed = (
        P("pair", None, ("row", "col")),
        P(None, ("row", "col")),
        P("pair", ("row", "col")),
        P(),
        P(("row", "col")),
    )
    out = (P("pair", None, ("row", "col")), P("pair", ("row", "col")))

    def whole(coords, final_coords, growth, counts, labels):
        cells = coords.shape[2]
        blocks = mesh.shape["row"] * mesh.shape["col"]
        fits = (
            2 * cells == LANES * blocks
            and blocks % 2 == 0
            and coords.shape[0] == mesh.shape["pair"]
            and HALF < coords.shape[1] < 2 * HALF - 1
            and 4 * cells * cells <= FUSED_BYTES
        )
        body = per_device_fused if fits else per_device
        return jax.shard_map(
            body, mesh=mesh, in_specs=placed, out_specs=out, check_vma=False
        )(coords, final_coords, growth, counts, labels)

    return whole
```

profile of v0, /device:TPU:0, one launch (start us, length us, event | category | flops | bytes accessed | tf_op | source)
XLA Modules:
  0.0 17.5 jit_solution(8767900886131284702)
XLA Ops:
  0.6 15.7 %shard_map.68 = (f32[1,16,64]{2,1,0:T(8,128)S(1)}, f32[1,64]{1,0:T(1,128)S(1)}) custom-call(s32[5]{0:T(128)} %counts_ref.1, f32[30,1,64]{2,1,0:T(1,128)} %bitcast.2, f32[30,64]{1,0:T(8,128)} %final_in.1, f32[1,64]{1,0:T(1,128)} %growth_in.1, s32[1,64]{1,0:T(1,128)} %bitcast.3), custom_call_target="tpu_custom_call" | custom-call | tf_op jit(solution)/shard_map/pallas_call | solution.py:428
  16.4 0.6 %copy.9 = f32[1,16,64]{2,1,0:T(8,128)} copy(f32[1,16,64]{2,1,0:T(8,128)S(1)} %get-tuple-element.2) | data formatting | bytes 8192
  17.0 0.5 %copy.10 = f32[1,64]{1,0:T(1,128)} copy(f32[1,64]{1,0:T(1,128)S(1)} %get-tuple-element.3) | data formatting | bytes 512
where the time goes:
time: 17.7 us; the launch traced here: 17.5 us
  Pallas kernels  15.7 us (89%)
  local copies, waits for them, and re-layouts  1.11 us (6%)
  between operations  0.64 us (4%)
    pallas_call x1, Pallas kernels, per_device_fused(): pl.pallas_call(functools.partial(fused, (n_pair, n_row, n_col, tile)), ou...  15.7 us
    unnamed x2, local copies, waits for them, and re-layouts  1.11 us

commit v1 on v0

v1 whole, which is shorter than its diff:
```python
import functools
import jax
import jax.numpy as jnp
from jax import lax
from jax.experimental import pallas as pl
from jax.experimental.pallas import tpu as pltpu
from jax.sharding import PartitionSpec as P

CLASSES = 16
FUSED_BYTES = 16 * 1024 * 1024


cost_scale = 1.0
source_power = 0.5
target_power = 50.0 / 51.0


def shifted_2(block, axis, distance):
    devices = range(lax.axis_size(axis))
    route = [(i - distance, i) for i in devices if i - distance in devices]
    return lax.ppermute(block, axis, route)


def kernel_tile(sources, targets):
    cross = lax.dot_general(
        sources,
        targets,
        (((0,), (0,)), ((), ())),
        precision=lax.Precision.HIGHEST,
        preferred_element_type=jnp.float32,
    )
    source_norms = jnp.sum(sources * sources, axis=0)
    target_norms = jnp.sum(targets * targets, axis=0)
    return jnp.exp(-(source_norms[:, None] + target_norms[None, :] - 2.0 * cross) / cost_scale)


def forward(kernel, weights):
    return lax.dot_general(
        weights,
        kernel,
        (((1,), (1,)), ((), ())),
        precision=lax.Precision.HIGHEST,
        preferred_element_type=jnp.float32,
    )


def backward(kernel, scales):
    return jnp.dot(
        scales, kernel, precision=lax.Precision.HIGHEST, preferred_element_type=jnp.float32
    )


def per_device(coords, final_coords, growth, counts, labels):
    tile = coords.shape[2]
    n_pair = lax.axis_size("pair")
    n_row = lax.axis_size("row")
    n_col = lax.axis_size("col")
    pair_at = lax.axis_index("pair")
    row_at = lax.axis_index("row")
    col_at = lax.axis_index("col")
    source_count = n_col * tile
    target_count = n_row * tile
    own_coords = coords[0]
    sources, source_growth = (
        lax.all_gather(own_coords, "col", axis=1, tiled=True),
        lax.all_gather(growth[0], "col", axis=0, tiled=True),
    )
    shifted = shifted_2(own_coords, "pair", -1)
    is_last = pair_at == n_pair - 1
    own_targets = jnp.where(is_last, final_coords, shifted)
    label_values = labels.astype(jnp.float32)
    position = lax.iota(jnp.int32, target_count)
    targets, target_labels = (
        lax.all_gather(own_targets, "row", axis=1, tiled=True),
        lax.all_gather(label_values, "row", axis=0, tiled=True),
    )
    target_index = position // tile * (n_col * tile) + col_at * tile + position % tile

    def hand_over(fates_now):
        incoming = shifted_2(fates_now, "pair", -1)
        return lax.all_gather(incoming, "row", axis=1, tiled=True)

    source_number = counts[pair_at]
    target_number = counts[pair_at + 1]
    source_total = source_number.astype(jnp.float32)
    target_total = target_number.astype(jnp.float32)
    source_index = row_at * source_count + lax.iota(jnp.int32, source_count)
    source_valid = source_index < source_number
    target_valid = target_index < target_number
    kernel = kernel_tile(sources, targets)
    start_terms = forward(kernel, target_valid.astype(jnp.float32)[None, :])[0]
    start_rows = lax.psum(start_terms, "col")
    source_mass = jnp.where(source_valid, source_growth / source_total, 0.0)
    scale_u = jnp.where(source_valid, jnp.power(source_mass / start_rows, source_power), 0.0)
    column_terms = backward(kernel, scale_u)
    column_totals = lax.psum(column_terms, "row")
    target_mass = target_valid.astype(jnp.float32) / target_total
    scale_v = jnp.where(target_valid, jnp.power(target_mass / column_totals, target_power), 0.0)
    own_offset = col_at * tile
    own_valid = lax.dynamic_slice_in_dim(source_valid, own_offset, tile, 0)
    own_scale = lax.dynamic_slice_in_dim(scale_u, own_offset, tile, 0)
    class_values = lax.iota(jnp.int32, CLASSES).astype(jnp.float32)
    label_table = jnp.where(
        (target_labels[None, :] == class_values[:, None]) & target_valid[None, :], 1.0, 0.0
    ).astype(jnp.float32)
    empty = jnp.zeros((CLASSES, tile), jnp.float32)
    final_terms = forward(kernel, scale_v[None, :])[0]
    final_rows = lax.psum(final_terms, "col")
    own_rows = lax.dynamic_slice_in_dim(final_rows, own_offset, tile, 0)
    safe_rows = jnp.where(own_valid, own_rows, 1.0)

    def advance(turn, fates_now):
        carried = jnp.where(is_last, label_table, hand_over(fates_now))
        terms = forward(kernel, carried * scale_v[None, :])
        sums = lax.psum_scatter(terms, "col", scatter_dimension=1, tiled=True)
        return jnp.where(own_valid[None, :], sums / safe_rows[None, :], 0.0)

    fates = lax.fori_loop(0, n_pair, advance, empty)
    mass = jnp.where(own_valid, source_total * own_scale * own_rows, 0.0)
    return (fates[None], mass[None])


LANES = 128
PIECES = 32
HALF = 16
BIG = 1e30
LOG2E = 1.4426950408889634
MESH = pl.DeviceIdType.MESH


def split3(a):
    first = a.astype(jnp.bfloat16)
    rest = a - first.astype(jnp.float32)
    second = rest.astype(jnp.bfloat16)
    third = (rest - second.astype(jnp.float32)).astype(jnp.bfloat16)
    return first, second, third


def split2(a):
    first = a.astype(jnp.bfloat16)
    return first, (a - first.astype(jnp.float32)).astype(jnp.bfloat16)


def dot(a, b, dims):
    return lax.dot_general(a, b, (dims, ((), ())), preferred_element_type=jnp.float32)


def packed(block, extra):
    low = block[:HALF]
    rest = block.shape[0] - HALF
    fill = jnp.zeros((HALF - rest - 1, block.shape[1]), jnp.float32)
    high = jnp.concatenate([block[HALF:], extra, fill], axis=0)
    return jnp.concatenate([low, high], axis=1)


def unpacked(ref, time, n_block):
    lows, highs = [], []
    lane = lax.broadcasted_iota(jnp.int32, (HALF, LANES), 1)
    for slot in range(0, n_block, 2):
        a, b = ref[time * n_block + slot], ref[time * n_block + slot + 1]
        swap_a, swap_b = pltpu.roll(a, LANES // 2, 1), pltpu.roll(b, LANES // 2, 1)
        lows.append(jnp.where(lane < LANES // 2, a, swap_b))
        highs.append(jnp.where(lane < LANES // 2, swap_a, b))
    low, high = jnp.concatenate(lows, axis=1), jnp.concatenate(highs, axis=1)
    return jnp.concatenate([low, high], axis=0)


def fused(
    sizes,
    counts_in,
    coords_in,
    final_in,
    growth_in,
    labels_in,
    fates_ref,
    mass_ref,
    counts_ref,
    coords_ref,
    final_ref,
    growth_ref,
    labels_ref,
    xg,
    k1,
    k2,
    fin,
    fout,
    own_sems,
    x_send,
    r_send,
    r_recv,
    x_recv,
    f_send,
    f_recv,
    ready,
):
    n_pair, n_row, n_col, tile = sizes
    n_block = n_row * n_col
    cells = n_block * tile
    pca = coords_in.shape[0]
    pair_at = lax.axis_index("pair")
    row_at = lax.axis_index("row")
    col_at = lax.axis_index("col")

    def place(slot):
        along, down = divmod(slot, n_row)
        return (row_at + down) % n_row, (col_at + along) % n_col

    barrier = pltpu.get_barrier_semaphore()
    mine = col_at * n_row + row_at

    def fed(pair):
        return [other for other in range(pair + 1) if other == pair or other % 2]

    def feeding(pair):
        return [other for other in range(n_pair) if pair in fed(other)]

    def met(pair):
        return [other for other in range(n_pair) if other in fed(pair) + feeding(pair)]

    def at(block):
        return block % n_row, block // n_row

    def signal(semaphore, pair, block):
        pl.semaphore_signal(
            semaphore, inc=1, device_id=(pair, *at(block)), device_id_type=MESH
        )

    def loop(start, stop, act):
        def step(block, carry):
            act(block)
            return carry

        lax.fori_loop(start, stop, step, 0)

    count_load = pltpu.make_async_copy(counts_in, counts_ref, own_sems.at[4])
    own_loads = (
        pltpu.make_async_copy(coords_in, coords_ref, own_sems.at[0]),
        pltpu.make_async_copy(growth_in, growth_ref, own_sems.at[1]),
        pltpu.make_async_copy(final_in, final_ref, own_sems.at[2]),
        pltpu.make_async_copy(labels_in, labels_ref, own_sems.at[3]),
    )
    for load in own_loads:
        load.start()
    count_load.start()

    def block_copy(time, pair, block):
        row, col = at(block)
        there = (col_at - col) % n_col * n_row + (row_at - row) % n_row
        return pltpu.make_async_remote_copy(
            src_ref=xg.at[time * n_block],
            dst_ref=xg.at[time * n_block + there],
            send_sem=x_send,
            recv_sem=x_recv.at[time],
            device_id=(pair, row, col),
            device_id_type=MESH,
        )

    below = jnp.maximum(pair_at - 1, 0)

    def blocks(time, start, number):
        return xg.at[pl.ds(time * n_block + start, number)]

    def relay(time):
        return pltpu.make_async_remote_copy(
            src_ref=blocks(time, 0, 2 * n_block),
            dst_ref=blocks(time, 0, 2 * n_block),
            send_sem=r_send,
            recv_sem=r_recv,
            device_id=(below, row_at, col_at),
            device_id_type=MESH,
        )

    f_copy = pltpu.make_async_remote_copy(
        src_ref=fout,
        dst_ref=fin,
        send_sem=f_send,
        recv_sem=f_recv,
        device_id=(below, row_at, col_at),
        device_id_type=MESH,
    )

    def arrival(buffer, sem):
        return pltpu.make_async_remote_copy(
            src_ref=buffer,
            dst_ref=buffer,
            send_sem=x_send,
            recv_sem=sem,
            device_id=(pair_at, row_at, col_at),
            device_id_type=MESH,
        )

    def bound(own, pair):
        shift = n_row * (own // 2 - pair // 2) + (pair < own)
        return jnp.minimum(jnp.maximum(mine + shift, 0), n_block)

    def send(own, is_upper):
        for pair in fed(own):

            def step(block, pair=pair):
                block_copy(own, pair, block).start()
                if pair == own and own % 2:
                    block_copy(n_pair, pair, block).start()

            if is_upper:
                loop(mine + 1 if pair == own else bound(own, pair), n_block, step)
            else:
                loop(0, mine if pair == own else bound(own, pair), step)

    def body(first):
        for pair in met(first):
            start = mine + 1 if pair == first else bound(first, pair)
            loop(start, n_block, functools.partial(signal, barrier, pair))
        if first % 2 == 0:
            signal(barrier, first + 1, mine)
        under = sum(mine if pair == first else bound(first, pair) for pair in met(first))
        if first % 2:
            pl.semaphore_wait(barrier, under + 1)
        else:
            pl.when(under > 0)(lambda: pl.semaphore_wait(barrier, under))
        for pair in feeding(first):
            stop = mine if pair == first else bound(first, pair)
            loop(0, stop, functools.partial(signal, ready, pair))
        for load in own_loads:
            load.wait()
        xg[first * n_block] = packed(coords_ref[:, 0, :], growth_ref[...])
        if first % 2:
            xg[n_pair * n_block] = packed(final_ref[...], labels_ref[...].astype(jnp.float32))
        send(first, False)
        over = sum(
            n_block - (mine + 1 if pair == first else bound(first, pair)) for pair in fed(first)
        )
        pl.when(over > 0)(lambda: pl.semaphore_wait(ready, over))
        send(first, True)
        count_load.wait()
        odd = first % 2 == 1
        stop = n_pair if odd else first + 2
        for time in range(first, n_pair + 1 if odd else first + 1):
            start = 1 if time in (first, n_pair) else 0
            arrival(blocks(time, start, n_block - start), x_recv.at[time]).wait_recv()
        if odd:
            relay(first).start()
        else:
            arrival(blocks(first + 1, 0, 2 * n_block), r_recv).wait_recv()

        lane = lax.broadcasted_iota(jnp.int32, (1, LANES), 1)
        pieces = []
        for slot in range(0, n_block, 2):
            bases = []
            for part in (slot, slot + 1):
                row, col = place(part)
                bases.append((row * n_col + col) * tile)
            pieces.append(jnp.where(lane < tile, bases[0] + lane, bases[1] + lane - tile))
        index = jnp.concatenate(pieces, axis=1)
        feature = lax.broadcasted_iota(jnp.int32, (PIECES, cells), 0)

        def joined(parts):
            return jnp.concatenate(list(parts), axis=1)

        lefts, rights, valid, extra = {}, {}, {}, {}
        for time in range(first, stop + 1):
            valid[time] = index < counts_ref[time]
            z = unpacked(xg, time, n_block)
            extra[time] = z[pca : pca + 1]
            z = jnp.where(feature < pca, z, 0.0)
            norm = jnp.sum(z * z, axis=0, keepdims=True) * LOG2E
            if time < stop:
                a = jnp.where(
                    feature < pca, z * (2.0 * LOG2E), jnp.where(feature == pca, -norm, 1.0)
                )
                a1, a2, a3 = split3(a)
                rights[time] = jnp.concatenate([a1, a2, a1, a2, a3, a1], axis=0)
            if time > first:
                low = jnp.where(valid[time], -norm, -BIG)
                b = jnp.where(feature < pca, z, jnp.where(feature == pca, 1.0, low))
                b1, b2, b3 = split3(b)
                lefts[time] = jnp.concatenate([b1, b1, b2, b2, b1, b3], axis=0)

        def numbers(time):
            return counts_ref[time].astype(jnp.float32)

        def plan(pair):
            total = jnp.zeros((8, cells), jnp.float32)
            for j in range(cells // LANES):
                rows = slice(j * LANES, (j + 1) * LANES)
                values = jnp.exp2(dot(lefts[pair + 1][:, rows], rights[pair], ((0,), (0,))))
                for k in range(LANES // 8):
                    total = total + values[k * 8 : (k + 1) * 8]
                high, low = split2(values)
                k1[pair, rows, :] = high
                k2[pair, rows, :] = low
            total = jnp.sum(total, axis=0, keepdims=True)
            share = jnp.sqrt(extra[pair] / numbers(pair))
            scale_u = jnp.where(valid[pair], share * lax.rsqrt(total), 0.0)
            u1, u2 = split2(jnp.broadcast_to(scale_u, (CLASSES, cells)))
            column = dot(jnp.concatenate([u1, u2], axis=0), k1[pair], ((1,), (1,)))
            column_low = dot(u1, k2[pair], ((1,), (1,)))
            column = column[:1] + column[CLASSES : CLASSES + 1] + column_low[:1]
            column = jnp.where(valid[pair + 1], column, 1.0)
            power = jnp.log2(column) + jnp.log2(jnp.full((1, cells), numbers(pair + 1)))
            scale_v = jnp.where(valid[pair + 1], jnp.exp2(-target_power * power), 0.0)
            row_totals = transported(pair, jnp.broadcast_to(scale_v, (CLASSES, cells)), cells)[:1]
            return scale_u, scale_v, row_totals

        def transported(pair, weights, width):
            w1, w2 = split2(weights)
            both = dot(jnp.concatenate([w1, w2], axis=0), k1[pair, :, :width], ((1,), (0,)))
            half = weights.shape[0]
            return both[:half] + both[half:] + dot(w1, k2[pair, :, :width], ((1,), (0,)))

        def advance(pair, scale_v, row_totals, fates):
            width = LANES if pair == first else cells
            share = jnp.where(valid[pair], 1.0 / row_totals, 0.0)
            return transported(pair, fates * scale_v, width) * share[:, :width]

        plans = {}
        if stop == n_pair:
            classes = lax.broadcasted_iota(jnp.int32, (CLASSES, cells), 0).astype(jnp.float32)
            fates = jnp.where((extra[n_pair] == classes) & valid[n_pair], 1.0, 0.0)
        for pair in range(stop - 1, first, -1):
            plans[pair] = plan(pair)
        if stop < n_pair:
            plans[first] = plan(first)
            f_copy.wait_recv()
            fates = fin[...]
        for pair in range(stop - 1, first, -1):
            fates = advance(pair, plans[pair][1], plans[pair][2], fates)
        if odd and first + 1 < n_pair:
            fout[...] = fates
            f_copy.start()
        if stop == n_pair:
            plans[first] = plan(first)
        scale_u, scale_v, row_totals = plans[first]
        fates = advance(first, scale_v, row_totals, fates)
        mass = jnp.where(valid[first], numbers(first) * scale_u * row_totals, 0.0)
        fates_ref[0] = fates[:, :tile]
        mass_ref[...] = mass[:, :tile]
        if odd:
            relay(first).wait_send()
            if first + 1 < n_pair:
                f_copy.wait_send()
        number = len(fed(first)) * n_block - 1 + (n_block - 1) * odd
        arrival(blocks(0, 0, number), x_recv.at[0]).wait_send()

    for pair in range(n_pair):

        @pl.when(pair_at == pair)
        def _(pair=pair):
            body(pair)


def per_device_fused(coords, final_coords, growth, counts, labels):
    pca, tile = coords.shape[1], coords.shape[2]
    n_pair = lax.axis_size("pair")
    n_row = lax.axis_size("row")
    n_col = lax.axis_size("col")
    n_block = n_row * n_col
    cells = n_block * tile
    vmem = pl.BlockSpec(memory_space=pltpu.VMEM)
    dma = pltpu.SemaphoreType.DMA
    return pl.pallas_call(
        functools.partial(fused, (n_pair, n_row, n_col, tile)),
        out_shape=(
            pltpu.VMEM((1, CLASSES, tile), jnp.float32),
            pltpu.VMEM((1, tile), jnp.float32),
        ),
        in_specs=[pl.BlockSpec(memory_space=pl.ANY)] * 5,
        out_specs=(vmem, vmem),
        scratch_shapes=[
            pltpu.SMEM((n_pair + 1,), jnp.int32),
            pltpu.VMEM((pca, 1, tile), jnp.float32),
            pltpu.VMEM((pca, tile), jnp.float32),
            pltpu.VMEM((1, tile), jnp.float32),
            pltpu.VMEM((1, tile), jnp.int32),
            pltpu.VMEM(((n_pair + 1) * n_block, HALF, LANES), jnp.float32),
            pltpu.VMEM((n_pair, cells, cells), jnp.bfloat16),
            pltpu.VMEM((n_pair, cells, cells), jnp.bfloat16),
            pltpu.VMEM((CLASSES, cells), jnp.float32),
            pltpu.VMEM((CLASSES, cells), jnp.float32),
            dma((5,)),
            dma,
            dma,
            dma,
            dma((n_pair + 1,)),
            dma,
            dma,
            pltpu.SemaphoreType.REGULAR,
        ],
        compiler_params=pltpu.CompilerParams(collective_id=0, has_side_effects=True),
    )(counts, jnp.transpose(coords, (1, 0, 2)), final_coords, growth, labels[None, :])


def solution(mesh):
    placed = (
        P("pair", None, ("row", "col")),
        P(None, ("row", "col")),
        P("pair", ("row", "col")),
        P(),
        P(("row", "col")),
    )
    out = (P("pair", None, ("row", "col")), P("pair", ("row", "col")))

    def whole(coords, final_coords, growth, counts, labels):
        cells = coords.shape[2]
        pairs = mesh.shape["pair"]
        blocks = mesh.shape["row"] * mesh.shape["col"]
        fits = (
            2 * cells == LANES * blocks
            and blocks % 2 == 0
            and pairs % 2 == 0
            and coords.shape[0] == pairs
            and coords.shape[1] + 2 <= PIECES
            and 4 * pairs * cells * cells <= FUSED_BYTES
        )
        body = per_device_fused if fits else per_device
        return jax.shard_map(
            body, mesh=mesh, in_specs=placed, out_specs=out, check_vma=False
        )(coords, final_coords, growth, counts, labels)

    return whole
```

time: 17.7 us -> 15.5 us (0.88)
  Pallas kernels: 15.7 us -> 13.5 us
    pallas_call x1, Pallas kernels: 15.7 us -> 13.5 us  [per_device_fused(): pl.pallas_call(functools.partial(fused, (n_pair, n_row, n_col, tile)), ou...]
where the time goes in v1:
time: 15.5 us; the launch traced here: 15.3 us
  Pallas kernels  13.5 us (87%)
  local copies, waits for them, and re-layouts  1.11 us (7%)
  between operations  0.64 us (4%)
    pallas_call x1, Pallas kernels, per_device_fused(): pl.pallas_call(functools.partial(fused, (n_pair, n_row, n_col, tile)), ou...  13.5 us
    unnamed x2, local copies, waits for them, and re-layouts  1.11 us

profile of v1, /device:TPU:0, one launch (start us, length us, event | category | flops | bytes accessed | tf_op | source)
XLA Modules:
  0.0 15.3 jit_solution(2569788395396783205)
XLA Ops:
  0.6 13.5 %shard_map.68 = (f32[1,16,64]{2,1,0:T(8,128)S(1)}, f32[1,64]{1,0:T(1,128)S(1)}) custom-call(s32[5]{0:T(128)} %counts_in.1, f32[30,1,64]{2,1,0:T(1,128)} %bitcast.2, f32[30,64]{1,0:T(8,128)} %final_in.1, f32[1,64]{1,0:T(1,128)} %growth_in.1, s32[1,64]{1,0:T(1,128)} %bitcast.3), custom_call_target="tpu_custom_call" | custom-call | tf_op jit(solution)/shard_map/pallas_call | solution.py:460
  14.1 0.6 %copy.9 = f32[1,16,64]{2,1,0:T(8,128)} copy(f32[1,16,64]{2,1,0:T(8,128)S(1)} %get-tuple-element.2) | data formatting | bytes 8192
  14.7 0.5 %copy.10 = f32[1,64]{1,0:T(1,128)} copy(f32[1,64]{1,0:T(1,128)S(1)} %get-tuple-element.3) | data formatting | bytes 512

commit v2 on v1

--- a/solution.py
+++ b/solution.py
@@ -448,6 +448,17 @@
             body(pair)
 
 
+def written(fates_ref, mass_ref, fates_out, mass_out, sems):
+    copies = (
+        pltpu.make_async_copy(mass_ref, mass_out, sems.at[0]),
+        pltpu.make_async_copy(fates_ref, fates_out, sems.at[1]),
+    )
+    for copy in copies:
+        copy.start()
+    for copy in copies:
+        copy.wait()
+
+
 def per_device_fused(coords, final_coords, growth, counts, labels):
     pca, tile = coords.shape[1], coords.shape[2]
     n_pair = lax.axis_size("pair")
@@ -457,7 +468,7 @@
     cells = n_block * tile
     vmem = pl.BlockSpec(memory_space=pltpu.VMEM)
     dma = pltpu.SemaphoreType.DMA
-    return pl.pallas_call(
+    fates, mass = pl.pallas_call(
         functools.partial(fused, (n_pair, n_row, n_col, tile)),
         out_shape=(
             pltpu.VMEM((1, CLASSES, tile), jnp.float32),
@@ -487,6 +498,16 @@
         ],
         compiler_params=pltpu.CompilerParams(collective_id=0, has_side_effects=True),
     )(counts, jnp.transpose(coords, (1, 0, 2)), final_coords, growth, labels[None, :])
+    return pl.pallas_call(
+        written,
+        out_shape=(
+            jax.ShapeDtypeStruct(fates.shape, jnp.float32),
+            jax.ShapeDtypeStruct(mass.shape, jnp.float32),
+        ),
+        in_specs=(vmem, vmem),
+        out_specs=(pl.BlockSpec(memory_space=pl.ANY), pl.BlockSpec(memory_space=pl.ANY)),
+        scratch_shapes=[dma((2,))],
+    )(*(pltpu.with_memory_space_constraint(x, pltpu.VMEM) for x in (fates, mass)))
 
 
 def solution(mesh):

time: 15.5 us -> 15 us (0.968)
  local copies, waits for them, and re-layouts: 1.11 us -> 0 us
  Pallas kernels: 13.5 us -> 14.1 us
    unnamed x2 -> x0, local copies, waits for them, and re-layouts: 1.11 us -> none
    pallas_call x0 -> x1, Pallas kernels: none -> 0.62 us  [per_device_fused(): pl.pallas_call(written, out_shape=(jax.ShapeDtypeStruct(fates.shape, jnp....]
where the time goes in v2:
time: 15 us; the launch traced here: 14.8 us
  Pallas kernels  14.1 us (94%)
  between operations  0.64 us (4%)
    pallas_call x1, Pallas kernels, per_device_fused(): pl.pallas_call(functools.partial(fused, (n_pair, n_row, n_col, tile)), ou...  13.5 us
    pallas_call x1, Pallas kernels, per_device_fused(): pl.pallas_call(written, out_shape=(jax.ShapeDtypeStruct(fates.shape, jnp....  0.62 us

profile of v2, /device:TPU:0, one launch (start us, length us, event | category | flops | bytes accessed | tf_op | source)
XLA Modules:
  0.0 14.8 jit_solution(3942084484749045519)
XLA Ops:
  0.6 13.5 %shard_map.68 = (f32[1,16,64]{2,1,0:T(8,128)S(1)}, f32[1,64]{1,0:T(1,128)S(1)}) custom-call(s32[5]{0:T(128)} %counts_in.1, f32[30,1,64]{2,1,0:T(1,128)} %bitcast.2, f32[30,64]{1,0:T(8,128)} %final_in.1, f32[1,64]{1,0:T(1,128)} %growth_in.1, s32[1,64]{1,0:T(1,128)} %bitcast.3), custom_call_target="tpu_custom_call" | custom-call | tf_op jit(solution)/shard_map/pallas_call | solution.py:471
  14.1 0.6 %shard_map.69 = (f32[1,16,64]{2,1,0:T(8,128)}, f32[1,64]{1,0:T(1,128)}) custom-call(f32[1,16,64]{2,1,0:T(8,128)S(1)} %get-tuple-element.4.fates_ref, f32[1,64]{1,0:T(1,128)S(1)} %get-tuple-element.5.mass_ref), custom_call_target="tpu_custom_call" | custom-call | tf_op jit(solution)/shard_map/pallas_call | solution.py:501

commit v3 on v2

--- a/solution.py
+++ b/solution.py
@@ -153,11 +153,11 @@
     return jnp.concatenate([low, high], axis=1)
 
 
-def unpacked(ref, time, n_block):
+def unpacked(ref, start, stop):
     lows, highs = [], []
     lane = lax.broadcasted_iota(jnp.int32, (HALF, LANES), 1)
-    for slot in range(0, n_block, 2):
-        a, b = ref[time * n_block + slot], ref[time * n_block + slot + 1]
+    for slot in range(start, stop, 2):
+        a, b = ref[slot], ref[slot + 1]
         swap_a, swap_b = pltpu.roll(a, LANES // 2, 1), pltpu.roll(b, LANES // 2, 1)
         lows.append(jnp.where(lane < LANES // 2, a, swap_b))
         highs.append(jnp.where(lane < LANES // 2, swap_a, b))
@@ -180,6 +180,7 @@
     growth_ref,
     labels_ref,
     xg,
+    kernel,
     k1,
     k2,
     fin,
@@ -187,7 +188,6 @@
     own_sems,
     x_send,
     r_send,
-    r_recv,
     x_recv,
     f_send,
     f_recv,
@@ -195,6 +195,7 @@
 ):
     n_pair, n_row, n_col, tile = sizes
     n_block = n_row * n_col
+    near = n_block - n_row
     cells = n_block * tile
     pca = coords_in.shape[0]
     pair_at = lax.axis_index("pair")
@@ -250,22 +251,25 @@
             src_ref=xg.at[time * n_block],
             dst_ref=xg.at[time * n_block + there],
             send_sem=x_send,
-            recv_sem=x_recv.at[time],
+            recv_sem=x_recv.at[time, there // near],
             device_id=(pair, row, col),
             device_id_type=MESH,
         )
 
+    parts = ((0, near), (near, n_block))
     below = jnp.maximum(pair_at - 1, 0)
 
     def blocks(time, start, number):
         return xg.at[pl.ds(time * n_block + start, number)]
 
-    def relay(time):
+    def relay(time, part):
+        start, stop = parts[part]
+        block = blocks(time, start, stop - start)
         return pltpu.make_async_remote_copy(
-            src_ref=blocks(time, 0, 2 * n_block),
-            dst_ref=blocks(time, 0, 2 * n_block),
+            src_ref=block,
+            dst_ref=block,
             send_sem=r_send,
-            recv_sem=r_recv,
+            recv_sem=x_recv.at[time, part],
             device_id=(below, row_at, col_at),
             device_id_type=MESH,
         )
@@ -279,18 +283,18 @@
         device_id_type=MESH,
     )
 
-    def arrival(buffer, sem):
+    def arrival(buffer, sem, send_sem=x_send):
         return pltpu.make_async_remote_copy(
             src_ref=buffer,
             dst_ref=buffer,
-            send_sem=x_send,
+            send_sem=send_sem,
             recv_sem=sem,
             device_id=(pair_at, row_at, col_at),
             device_id_type=MESH,
         )
 
     def bound(own, pair):
-        shift = n_row * (own // 2 - pair // 2) + (pair < own)
+        shift = 4 * n_row * (own // 2 - pair // 2) + (pair < own)
         return jnp.minimum(jnp.maximum(mine + shift, 0), n_block)
 
     def send(own, is_upper):
@@ -301,10 +305,13 @@
                 if pair == own and own % 2:
                     block_copy(n_pair, pair, block).start()
 
+            under = mine if pair == own else bound(own, pair)
+            early = jnp.minimum(under, 1)
             if is_upper:
-                loop(mine + 1 if pair == own else bound(own, pair), n_block, step)
+                loop(early, under, step)
+                loop(mine + 1 if pair == own else under, n_block, step)
             else:
-                loop(0, mine if pair == own else bound(own, pair), step)
+                loop(0, early, step)
 
     def body(first):
         for pair in met(first):
@@ -334,112 +341,149 @@
         count_load.wait()
         odd = first % 2 == 1
         stop = n_pair if odd else first + 2
-        for time in range(first, n_pair + 1 if odd else first + 1):
-            start = 1 if time in (first, n_pair) else 0
-            arrival(blocks(time, start, n_block - start), x_recv.at[time]).wait_recv()
-        if odd:
-            relay(first).start()
-        else:
-            arrival(blocks(first + 1, 0, 2 * n_block), r_recv).wait_recv()
-
         lane = lax.broadcasted_iota(jnp.int32, (1, LANES), 1)
         pieces = []
         for slot in range(0, n_block, 2):
             bases = []
-            for part in (slot, slot + 1):
-                row, col = place(part)
+            for one in (slot, slot + 1):
+                row, col = place(one)
                 bases.append((row * n_col + col) * tile)
             pieces.append(jnp.where(lane < tile, bases[0] + lane, bases[1] + lane - tile))
         index = jnp.concatenate(pieces, axis=1)
-        feature = lax.broadcasted_iota(jnp.int32, (PIECES, cells), 0)
-
-        def joined(parts):
-            return jnp.concatenate(list(parts), axis=1)
-
-        lefts, rights, valid, extra = {}, {}, {}, {}
-        for time in range(first, stop + 1):
-            valid[time] = index < counts_ref[time]
-            z = unpacked(xg, time, n_block)
-            extra[time] = z[pca : pca + 1]
-            z = jnp.where(feature < pca, z, 0.0)
-            norm = jnp.sum(z * z, axis=0, keepdims=True) * LOG2E
-            if time < stop:
-                a = jnp.where(
-                    feature < pca, z * (2.0 * LOG2E), jnp.where(feature == pca, -norm, 1.0)
-                )
-                a1, a2, a3 = split3(a)
-                rights[time] = jnp.concatenate([a1, a2, a1, a2, a3, a1], axis=0)
-            if time > first:
-                low = jnp.where(valid[time], -norm, -BIG)
-                b = jnp.where(feature < pca, z, jnp.where(feature == pca, 1.0, low))
-                b1, b2, b3 = split3(b)
-                lefts[time] = jnp.concatenate([b1, b1, b2, b2, b1, b3], axis=0)
-
-        def numbers(time):
-            return counts_ref[time].astype(jnp.float32)
-
-        def plan(pair):
-            total = jnp.zeros((8, cells), jnp.float32)
-            for j in range(cells // LANES):
-                rows = slice(j * LANES, (j + 1) * LANES)
-                values = jnp.exp2(dot(lefts[pair + 1][:, rows], rights[pair], ((0,), (0,))))
+        valid = {time: index < counts_ref[time] for time in range(first, stop + 1)}
+        numbers = {time: counts_ref[time].astype(jnp.float32) for time in range(first, stop + 1)}
+        lefts, rights, extras, totals = {}, {}, {}, {}
+
+        def arrive(part):
+            for time in range(first, stop + 1):
+                start, end = parts[part]
+                if part == 0 and (time == first or (odd and time == n_pair)):
+                    start = 1
+                arrival(blocks(time, start, end - start), x_recv.at[time, part]).wait_recv()
+                if odd and time < first + 2:
+                    relay(time, part).start()
+
+        def prepare(part):
+            start, end = parts[part]
+            width = (end - start) * tile
+            lanes = slice(start * tile, end * tile)
+            feature = lax.broadcasted_iota(jnp.int32, (PIECES, width), 0)
+            for time in range(first, stop + 1):
+                z = unpacked(xg, time * n_block + start, time * n_block + end)
+                extras[time, part] = z[pca : pca + 1]
+                z = jnp.where(feature < pca, z, 0.0)
+                norm = jnp.sum(z * z, axis=0, keepdims=True) * LOG2E
+                if time < stop:
+                    a = jnp.where(
+                        feature < pca, z * (2.0 * LOG2E), jnp.where(feature == pca, -norm, 1.0)
+                    )
+                    a1, a2, a3 = split3(a)
+                    rights[time, part] = jnp.concatenate([a1, a2, a1, a2, a3, a1], axis=0)
+                if time > first:
+                    low = jnp.where(valid[time][:, lanes], -norm, -BIG)
+                    b = jnp.where(feature < pca, z, jnp.where(feature == pca, 1.0, low))
+                    b1, b2, b3 = split3(b)
+                    lefts[time, part] = jnp.concatenate([b1, b1, b2, b2, b1, b3], axis=0)
+
+        def fill(pair, part, other):
+            first_row, first_lane = parts[part][0] * tile, parts[other][0] * tile
+            left, right = lefts[pair + 1, part], rights[pair, other]
+            lanes = slice(first_lane, first_lane + right.shape[1])
+            total = totals.get((pair, other), jnp.zeros((8, right.shape[1]), jnp.float32))
+            for j in range(left.shape[1] // LANES):
+                values = jnp.exp2(dot(left[:, j * LANES : (j + 1) * LANES], right, ((0,), (0,))))
                 for k in range(LANES // 8):
                     total = total + values[k * 8 : (k + 1) * 8]
-                high, low = split2(values)
-                k1[pair, rows, :] = high
-                k2[pair, rows, :] = low
-            total = jnp.sum(total, axis=0, keepdims=True)
-            share = jnp.sqrt(extra[pair] / numbers(pair))
-            scale_u = jnp.where(valid[pair], share * lax.rsqrt(total), 0.0)
-            u1, u2 = split2(jnp.broadcast_to(scale_u, (CLASSES, cells)))
-            column = dot(jnp.concatenate([u1, u2], axis=0), k1[pair], ((1,), (1,)))
-            column_low = dot(u1, k2[pair], ((1,), (1,)))
-            column = column[:1] + column[CLASSES : CLASSES + 1] + column_low[:1]
-            column = jnp.where(valid[pair + 1], column, 1.0)
-            power = jnp.log2(column) + jnp.log2(jnp.full((1, cells), numbers(pair + 1)))
-            scale_v = jnp.where(valid[pair + 1], jnp.exp2(-target_power * power), 0.0)
-            row_totals = transported(pair, jnp.broadcast_to(scale_v, (CLASSES, cells)), cells)[:1]
-            return scale_u, scale_v, row_totals
-
-        def transported(pair, weights, width):
-            w1, w2 = split2(weights)
-            both = dot(jnp.concatenate([w1, w2], axis=0), k1[pair, :, :width], ((1,), (0,)))
-            half = weights.shape[0]
-            return both[:half] + both[half:] + dot(w1, k2[pair, :, :width], ((1,), (0,)))
-
-        def advance(pair, scale_v, row_totals, fates):
-            width = LANES if pair == first else cells
-            share = jnp.where(valid[pair], 1.0 / row_totals, 0.0)
-            return transported(pair, fates * scale_v, width) * share[:, :width]
-
-        plans = {}
+                rows = slice(first_row + j * LANES, first_row + (j + 1) * LANES)
+                kernel[pair, rows, lanes] = values
+            totals[pair, other] = total
+
+        def extra(time):
+            return jnp.concatenate([extras[time, 0], extras[time, 1]], axis=1)
+
+        scale_u, row_totals = {}, {}
+        iota_rows = lax.broadcasted_iota(jnp.int32, (tile, 1), 0)
+
+        def settle(pairs):
+            for pair in pairs:
+                total = jnp.concatenate([totals[pair, 0], totals[pair, 1]], axis=1)
+                total = jnp.sum(total, axis=0, keepdims=True)
+                share = jnp.sqrt(extra(pair) / numbers[pair])
+                scale_u[pair] = jnp.where(valid[pair], share * lax.rsqrt(total), 0.0)
+            sums = {pair: jnp.zeros((8, cells), jnp.float32) for pair in pairs}
+            for slot in range(n_block):
+                rows = slice(slot * tile, (slot + 1) * tile)
+                row, col = place(slot)
+                position = (row * n_col + col) * tile + iota_rows
+                for pair in pairs:
+                    values = kernel[pair, rows, :]
+                    terms = values * scale_u[pair]
+                    folded = terms[:, :LANES]
+                    for j in range(1, cells // LANES):
+                        folded = folded + terms[:, j * LANES : (j + 1) * LANES]
+                    column = jnp.sum(folded, axis=1, keepdims=True)
+                    is_target = position < counts_ref[pair + 1]
+                    column = jnp.where(is_target, column, 1.0)
+                    power = jnp.log2(column) + jnp.log2(jnp.full((tile, 1), numbers[pair + 1]))
+                    scale_v = jnp.where(is_target, jnp.exp2(-target_power * power), 0.0)
+                    scaled = values * scale_v
+                    for k in range(tile // 8):
+                        sums[pair] = sums[pair] + scaled[k * 8 : (k + 1) * 8]
+                    high, low = split2(scaled)
+                    k1[pair, rows, :] = high
+                    k2[pair, rows, :] = low
+            for pair in pairs:
+                row_totals[pair] = jnp.sum(sums[pair], axis=0, keepdims=True)
+
+        def advance(pair, fates):
+            width = cells if pair > first else LANES
+            share = jnp.where(valid[pair], 1.0 / row_totals[pair], 0.0)
+            f1, f2 = split2(fates)
+            high, low = k1[pair, :, :width], k2[pair, :, :width]
+            sums = dot(jnp.concatenate([f1, f2], axis=0), high, ((1,), (0,)))
+            sums = sums[:CLASSES] + sums[CLASSES:] + dot(f1, low, ((1,), (0,)))
+            return sums * share[:, :width]
+
+        alone = odd and first + 1 < n_pair
+        lead = range(stop - 1, first if alone else first - 1, -1)
+        arrive(0)
+        prepare(0)
+        for pair in lead:
+            fill(pair, 0, 0)
+        arrive(1)
+        prepare(1)
+        for pair in lead:
+            fill(pair, 0, 1)
+            fill(pair, 1, 0)
+            fill(pair, 1, 1)
+        settle(lead)
         if stop == n_pair:
             classes = lax.broadcasted_iota(jnp.int32, (CLASSES, cells), 0).astype(jnp.float32)
-            fates = jnp.where((extra[n_pair] == classes) & valid[n_pair], 1.0, 0.0)
-        for pair in range(stop - 1, first, -1):
-            plans[pair] = plan(pair)
-        if stop < n_pair:
-            plans[first] = plan(first)
+            fates = jnp.where((extra(n_pair) == classes) & valid[n_pair], 1.0, 0.0)
+        else:
             f_copy.wait_recv()
             fates = fin[...]
         for pair in range(stop - 1, first, -1):
-            fates = advance(pair, plans[pair][1], plans[pair][2], fates)
-        if odd and first + 1 < n_pair:
+            fates = advance(pair, fates)
+        if alone:
             fout[...] = fates
             f_copy.start()
-        if stop == n_pair:
-            plans[first] = plan(first)
-        scale_u, scale_v, row_totals = plans[first]
-        fates = advance(first, scale_v, row_totals, fates)
-        mass = jnp.where(valid[first], numbers(first) * scale_u * row_totals, 0.0)
+            for part in range(2):
+                for other in range(2):
+                    fill(first, part, other)
+            settle([first])
+        fates = advance(first, fates)
+        mass = jnp.where(
+            valid[first], numbers[first] * scale_u[first] * row_totals[first], 0.0
+        )
         fates_ref[0] = fates[:, :tile]
         mass_ref[...] = mass[:, :tile]
         if odd:
-            relay(first).wait_send()
-            if first + 1 < n_pair:
+            arrival(blocks(first, 0, 2 * n_block), x_recv.at[0, 0], r_send).wait_send()
+            if alone:
                 f_copy.wait_send()
         number = len(fed(first)) * n_block - 1 + (n_block - 1) * odd
-        arrival(blocks(0, 0, number), x_recv.at[0]).wait_send()
+        arrival(blocks(0, 0, number), x_recv.at[0, 0]).wait_send()
 
     for pair in range(n_pair):
 
@@ -483,6 +527,7 @@
             pltpu.VMEM((1, tile), jnp.float32),
             pltpu.VMEM((1, tile), jnp.int32),
             pltpu.VMEM(((n_pair + 1) * n_block, HALF, LANES), jnp.float32),
+            pltpu.VMEM((n_pair, cells, cells), jnp.float32),
             pltpu.VMEM((n_pair, cells, cells), jnp.bfloat16),
             pltpu.VMEM((n_pair, cells, cells), jnp.bfloat16),
             pltpu.VMEM((CLASSES, cells), jnp.float32),
@@ -490,8 +535,7 @@
             dma((5,)),
             dma,
             dma,
-            dma,
-            dma((n_pair + 1,)),
+            dma((n_pair + 1, 2)),
             dma,
             dma,
             pltpu.SemaphoreType.REGULAR,
@@ -507,7 +551,7 @@
         in_specs=(vmem, vmem),
         out_specs=(pl.BlockSpec(memory_space=pl.ANY), pl.BlockSpec(memory_space=pl.ANY)),
         scratch_shapes=[dma((2,))],
-    )(*(pltpu.with_memory_space_constraint(x, pltpu.VMEM) for x in (fates, mass)))
+    )(*(pltpu.with_memory_space_constraint(array, pltpu.VMEM) for array in (fates, mass)))
 
 
 def solution(mesh):
@@ -526,11 +570,12 @@
         blocks = mesh.shape["row"] * mesh.shape["col"]
         fits = (
             2 * cells == LANES * blocks
-            and blocks % 2 == 0
+            and mesh.shape["row"] % 2 == 0
+            and mesh.shape["col"] > 1
             and pairs % 2 == 0
             and coords.shape[0] == pairs
             and coords.shape[1] + 2 <= PIECES
-            and 4 * pairs * cells * cells <= FUSED_BYTES
+            and 8 * pairs * cells * cells <= FUSED_BYTES
         )
         body = per_device_fused if fits else per_device
         return jax.shard_map(

time: 15 us -> 14.1 us (0.940)
  Pallas kernels: 14.1 us -> 13.2 us
    pallas_call x1, Pallas kernels: 13.5 us -> 12.6 us  [per_device_fused(): pl.pallas_call(functools.partial(fused, (n_pair, n_row, n_col, tile)), ou...]
where the time goes in v3:
time: 14.1 us; the launch traced here: 13.8 us
  Pallas kernels  13.2 us (94%)
  between operations  0.64 us (5%)
    pallas_call x1, Pallas kernels, per_device_fused(): pl.pallas_call(functools.partial(fused, (n_pair, n_row, n_col, tile)), ou...  12.6 us
    pallas_call x1, Pallas kernels, per_device_fused(): pl.pallas_call(written, out_shape=(jax.ShapeDtypeStruct(fates.shape, jnp....  0.62 us

profile of v3, /device:TPU:0, one launch (start us, length us, event | category | flops | bytes accessed | tf_op | source)
XLA Modules:
  0.0 13.8 jit_solution(3173476490246060905)
XLA Ops:
  0.6 12.6 %shard_map.68 = (f32[1,16,64]{2,1,0:T(8,128)S(1)}, f32[1,64]{1,0:T(1,128)S(1)}) custom-call(s32[5]{0:T(128)} %counts_in.1, f32[30,1,64]{2,1,0:T(1,128)} %bitcast.2, f32[30,64]{1,0:T(8,128)} %final_in.1, f32[1,64]{1,0:T(1,128)} %growth_in.1, s32[1,64]{1,0:T(1,128)} %bitcast.3), custom_call_target="tpu_custom_call" | custom-call | tf_op jit(solution)/shard_map/pallas_call | solution.py:515
  13.2 0.6 %shard_map.69 = (f32[1,16,64]{2,1,0:T(8,128)}, f32[1,64]{1,0:T(1,128)}) custom-call(f32[1,16,64]{2,1,0:T(8,128)S(1)} %get-tuple-element.4.fates_ref, f32[1,64]{1,0:T(1,128)S(1)} %get-tuple-element.5.mass_ref), custom_call_target="tpu_custom_call" | custom-call | tf_op jit(solution)/shard_map/pallas_call | solution.py:545

commit v4 on v3

--- a/solution.py
+++ b/solution.py
@@ -187,9 +187,7 @@
     fout,
     own_sems,
     x_send,
-    r_send,
     x_recv,
-    f_send,
     f_recv,
     ready,
 ):
@@ -268,7 +266,7 @@
         return pltpu.make_async_remote_copy(
             src_ref=block,
             dst_ref=block,
-            send_sem=r_send,
+            send_sem=x_send,
             recv_sem=x_recv.at[time, part],
             device_id=(below, row_at, col_at),
             device_id_type=MESH,
@@ -277,17 +275,17 @@
     f_copy = pltpu.make_async_remote_copy(
         src_ref=fout,
         dst_ref=fin,
-        send_sem=f_send,
+        send_sem=x_send,
         recv_sem=f_recv,
         device_id=(below, row_at, col_at),
         device_id_type=MESH,
     )
 
-    def arrival(buffer, sem, send_sem=x_send):
+    def arrival(buffer, sem):
         return pltpu.make_async_remote_copy(
             src_ref=buffer,
             dst_ref=buffer,
-            send_sem=send_sem,
+            send_sem=x_send,
             recv_sem=sem,
             device_id=(pair_at, row_at, col_at),
             device_id_type=MESH,
@@ -297,7 +295,13 @@
         shift = 4 * n_row * (own // 2 - pair // 2) + (pair < own)
         return jnp.minimum(jnp.maximum(mine + shift, 0), n_block)
 
-    def send(own, is_upper):
+    def inner(block):
+        row, col = at(block)
+        return (row > 0 and col > 0, -row - col, row)
+
+    order = sorted(range(1, n_block), key=inner)
+
+    def send(own, is_late):
         for pair in fed(own):
 
             def step(block, pair=pair):
@@ -305,13 +309,16 @@
                 if pair == own and own % 2:
                     block_copy(n_pair, pair, block).start()
 
-            under = mine if pair == own else bound(own, pair)
-            early = jnp.minimum(under, 1)
-            if is_upper:
-                loop(early, under, step)
-                loop(mine + 1 if pair == own else under, n_block, step)
-            else:
-                loop(0, early, step)
+            if not is_late:
+                pl.when((mine if pair == own else bound(own, pair)) > 0)(lambda: step(0))
+                continue
+            if pair < own:
+                pl.when(bound(own, pair) == 0)(lambda: step(0))
+            for block in order:
+                if pair < own:
+                    step(block)
+                else:
+                    pl.when(mine != block)(functools.partial(step, block))
 
     def body(first):
         for pair in met(first):
@@ -440,8 +447,12 @@
             share = jnp.where(valid[pair], 1.0 / row_totals[pair], 0.0)
             f1, f2 = split2(fates)
             high, low = k1[pair, :, :width], k2[pair, :, :width]
-            sums = dot(jnp.concatenate([f1, f2], axis=0), high, ((1,), (0,)))
-            sums = sums[:CLASSES] + sums[CLASSES:] + dot(f1, low, ((1,), (0,)))
+            if pair == n_pair - 1:
+                sums = dot(f1, high, ((1,), (0,)))
+            else:
+                sums = dot(jnp.concatenate([f1, f2], axis=0), high, ((1,), (0,)))
+                sums = sums[:CLASSES] + sums[CLASSES:]
+            sums = sums + dot(f1, low, ((1,), (0,)))
             return sums * share[:, :width]
 
         alone = odd and first + 1 < n_pair
@@ -478,11 +489,11 @@
         )
         fates_ref[0] = fates[:, :tile]
         mass_ref[...] = mass[:, :tile]
+        number = len(fed(first)) * n_block - 1 + (n_block - 1) * odd
         if odd:
-            arrival(blocks(first, 0, 2 * n_block), x_recv.at[0, 0], r_send).wait_send()
+            number = number + 2 * n_block
             if alone:
                 f_copy.wait_send()
-        number = len(fed(first)) * n_block - 1 + (n_block - 1) * odd
         arrival(blocks(0, 0, number), x_recv.at[0, 0]).wait_send()
 
     for pair in range(n_pair):
@@ -534,9 +545,7 @@
             pltpu.VMEM((CLASSES, cells), jnp.float32),
             dma((5,)),
             dma,
-            dma,
             dma((n_pair + 1, 2)),
-            dma,
             dma,
             pltpu.SemaphoreType.REGULAR,
         ],

time: 14.1 us -> 13.9 us (0.986)
  no operation moved by 1% of the time
where the time goes in v4:
time: 13.9 us; the launch traced here: 13.7 us
  Pallas kernels  13.1 us (94%)
  between operations  0.64 us (5%)
    pallas_call x1, Pallas kernels, per_device_fused(): pl.pallas_call(functools.partial(fused, (n_pair, n_row, n_col, tile)), ou...  12.4 us
    pallas_call x1, Pallas kernels, per_device_fused(): pl.pallas_call(written, out_shape=(jax.ShapeDtypeStruct(fates.shape, jnp....  0.62 us

profile of v4, /device:TPU:0, one launch (start us, length us, event | category | flops | bytes accessed | tf_op | source)
XLA Modules:
  0.0 13.7 jit_solution(15734926936718384321)
XLA Ops:
  0.6 12.4 %shard_map.68 = (f32[1,16,64]{2,1,0:T(8,128)S(1)}, f32[1,64]{1,0:T(1,128)S(1)}) custom-call(s32[5]{0:T(128)} %counts_in.1, f32[30,1,64]{2,1,0:T(1,128)} %bitcast.2, f32[30,64]{1,0:T(8,128)} %final_in.1, f32[1,64]{1,0:T(1,128)} %growth_in.1, s32[1,64]{1,0:T(1,128)} %bitcast.3), custom_call_target="tpu_custom_call" | custom-call | tf_op jit(solution)/shard_map/pallas_call | solution.py:526
  13.1 0.6 %shard_map.69 = (f32[1,16,64]{2,1,0:T(8,128)}, f32[1,64]{1,0:T(1,128)}) custom-call(f32[1,16,64]{2,1,0:T(8,128)S(1)} %get-tuple-element.4.fates_ref, f32[1,64]{1,0:T(1,128)S(1)} %get-tuple-element.5.mass_ref), custom_call_target="tpu_custom_call" | custom-call | tf_op jit(solution)/shard_map/pallas_call | solution.py:554

commit v5 on v4

--- a/solution.py
+++ b/solution.py
@@ -185,10 +185,12 @@
     k2,
     fin,
     fout,
+    results,
     own_sems,
     x_send,
     x_recv,
     f_recv,
+    result_recv,
     ready,
 ):
     n_pair, n_row, n_col, tile = sizes
@@ -207,15 +209,6 @@
     barrier = pltpu.get_barrier_semaphore()
     mine = col_at * n_row + row_at
 
-    def fed(pair):
-        return [other for other in range(pair + 1) if other == pair or other % 2]
-
-    def feeding(pair):
-        return [other for other in range(n_pair) if pair in fed(other)]
-
-    def met(pair):
-        return [other for other in range(n_pair) if other in fed(pair) + feeding(pair)]
-
     def at(block):
         return block % n_row, block // n_row
 
@@ -238,10 +231,6 @@
         pltpu.make_async_copy(final_in, final_ref, own_sems.at[2]),
         pltpu.make_async_copy(labels_in, labels_ref, own_sems.at[3]),
     )
-    for load in own_loads:
-        load.start()
-    count_load.start()
-
     def block_copy(time, pair, block):
         row, col = at(block)
         there = (col_at - col) % n_col * n_row + (row_at - row) % n_row
@@ -291,63 +280,70 @@
             device_id_type=MESH,
         )
 
-    def bound(own, pair):
-        shift = 4 * n_row * (own // 2 - pair // 2) + (pair < own)
-        return jnp.minimum(jnp.maximum(mine + shift, 0), n_block)
-
     def inner(block):
         row, col = at(block)
         return (row > 0 and col > 0, -row - col, row)
 
     order = sorted(range(1, n_block), key=inner)
 
-    def send(own, is_late):
-        for pair in fed(own):
-
-            def step(block, pair=pair):
-                block_copy(own, pair, block).start()
-                if pair == own and own % 2:
-                    block_copy(n_pair, pair, block).start()
-
-            if not is_late:
-                pl.when((mine if pair == own else bound(own, pair)) > 0)(lambda: step(0))
-                continue
-            if pair < own:
-                pl.when(bound(own, pair) == 0)(lambda: step(0))
-            for block in order:
-                if pair < own:
-                    step(block)
-                else:
-                    pl.when(mine != block)(functools.partial(step, block))
-
-    def body(first):
-        for pair in met(first):
-            start = mine + 1 if pair == first else bound(first, pair)
-            loop(start, n_block, functools.partial(signal, barrier, pair))
-        if first % 2 == 0:
-            signal(barrier, first + 1, mine)
-        under = sum(mine if pair == first else bound(first, pair) for pair in met(first))
-        if first % 2:
-            pl.semaphore_wait(barrier, under + 1)
-        else:
-            pl.when(under > 0)(lambda: pl.semaphore_wait(barrier, under))
-        for pair in feeding(first):
-            stop = mine if pair == first else bound(first, pair)
-            loop(0, stop, functools.partial(signal, ready, pair))
-        for load in own_loads:
+    def send(own, block):
+        block_copy(own, min(own, 1), block).start()
+        if own == 1:
+            block_copy(n_pair, 1, block).start()
+
+    def result_copy(pair):
+        return pltpu.make_async_remote_copy(
+            src_ref=results.at[pair],
+            dst_ref=results.at[pair],
+            send_sem=x_send,
+            recv_sem=result_recv,
+            device_id=(pair, row_at, col_at),
+            device_id_type=MESH,
+        )
+
+    def only_send(first):
+        for load in own_loads[:2]:
+            load.start()
+        for load in own_loads[:2]:
             load.wait()
         xg[first * n_block] = packed(coords_ref[:, 0, :], growth_ref[...])
-        if first % 2:
+        pl.semaphore_wait(barrier, n_block)
+        for block in [0, *order]:
+            send(first, block)
+        arrival(results.at[first], result_recv).wait_recv()
+        fates_ref[0] = results[first, :CLASSES, :tile]
+        mass_ref[...] = results[first, CLASSES : CLASSES + 1, :tile]
+        arrival(blocks(0, 0, n_block), x_recv.at[0, 0]).wait_send()
+
+    def body(first):
+        odd = first == 1
+        stop = n_pair if odd else 2
+        loads = (*own_loads[: 4 if odd else 2], count_load)
+        for load in loads:
+            load.start()
+        if odd:
+            for block in (*order, 0):
+                for pair in range(2, n_pair):
+                    signal(barrier, pair, block)
+        else:
+            signal(barrier, 1, mine)
+        loop(mine + 1, n_block, functools.partial(signal, barrier, first))
+        if odd:
+            pl.semaphore_wait(barrier, mine + 1)
+        else:
+            pl.when(mine > 0)(lambda: pl.semaphore_wait(barrier, mine))
+        loop(0, mine, functools.partial(signal, ready, first))
+        for load in loads[:-1]:
+            load.wait()
+        xg[first * n_block] = packed(coords_ref[:, 0, :], growth_ref[...])
+        if odd:
             xg[n_pair * n_block] = packed(final_ref[...], labels_ref[...].astype(jnp.float32))
-        send(first, False)
-        over = sum(
-            n_block - (mine + 1 if pair == first else bound(first, pair)) for pair in fed(first)
-        )
+        pl.when(mine > 0)(lambda: send(first, 0))
+        over = n_block - 1 - mine
         pl.when(over > 0)(lambda: pl.semaphore_wait(ready, over))
-        send(first, True)
+        for block in order:
+            pl.when(mine != block)(functools.partial(send, first, block))
         count_load.wait()
-        odd = first % 2 == 1
-        stop = n_pair if odd else first + 2
         lane = lax.broadcasted_iota(jnp.int32, (1, LANES), 1)
         pieces = []
         for slot in range(0, n_block, 2):
@@ -442,6 +438,10 @@
             for pair in pairs:
                 row_totals[pair] = jnp.sum(sums[pair], axis=0, keepdims=True)
 
+        def moved(pair):
+            mass = numbers[pair] * scale_u[pair] * row_totals[pair]
+            return jnp.where(valid[pair], mass, 0.0)
+
         def advance(pair, fates):
             width = cells if pair > first else LANES
             share = jnp.where(valid[pair], 1.0 / row_totals[pair], 0.0)
@@ -455,8 +455,7 @@
             sums = sums + dot(f1, low, ((1,), (0,)))
             return sums * share[:, :width]
 
-        alone = odd and first + 1 < n_pair
-        lead = range(stop - 1, first if alone else first - 1, -1)
+        lead = range(stop - 1, first if odd else first - 1, -1)
         arrive(0)
         prepare(0)
         for pair in lead:
@@ -468,39 +467,40 @@
             fill(pair, 1, 0)
             fill(pair, 1, 1)
         settle(lead)
-        if stop == n_pair:
+        if odd:
             classes = lax.broadcasted_iota(jnp.int32, (CLASSES, cells), 0).astype(jnp.float32)
             fates = jnp.where((extra(n_pair) == classes) & valid[n_pair], 1.0, 0.0)
         else:
             f_copy.wait_recv()
             fates = fin[...]
+        own = {}
         for pair in range(stop - 1, first, -1):
             fates = advance(pair, fates)
-        if alone:
+            own[pair] = fates[:, :LANES]
+        if odd:
             fout[...] = fates
             f_copy.start()
+            for pair in lead:
+                results[pair, :CLASSES] = own[pair]
+                results[pair, CLASSES:] = jnp.broadcast_to(moved(pair)[:, :LANES], (8, LANES))
+                result_copy(pair).start()
             for part in range(2):
                 for other in range(2):
                     fill(first, part, other)
             settle([first])
         fates = advance(first, fates)
-        mass = jnp.where(
-            valid[first], numbers[first] * scale_u[first] * row_totals[first], 0.0
-        )
         fates_ref[0] = fates[:, :tile]
-        mass_ref[...] = mass[:, :tile]
-        number = len(fed(first)) * n_block - 1 + (n_block - 1) * odd
+        mass_ref[...] = moved(first)[:, :tile]
+        number = n_block - 1
         if odd:
-            number = number + 2 * n_block
-            if alone:
-                f_copy.wait_send()
+            number = 2 * number + 2 * n_block
+            f_copy.wait_send()
+            for pair in lead:
+                result_copy(pair).wait_send()
         arrival(blocks(0, 0, number), x_recv.at[0, 0]).wait_send()
 
     for pair in range(n_pair):
-
-        @pl.when(pair_at == pair)
-        def _(pair=pair):
-            body(pair)
+        pl.when(pair_at == pair)(functools.partial(body if pair < 2 else only_send, pair))
 
 
 def written(fates_ref, mass_ref, fates_out, mass_out, sems):
@@ -543,9 +543,11 @@
             pltpu.VMEM((n_pair, cells, cells), jnp.bfloat16),
             pltpu.VMEM((CLASSES, cells), jnp.float32),
             pltpu.VMEM((CLASSES, cells), jnp.float32),
+            pltpu.VMEM((n_pair, CLASSES + 8, LANES), jnp.float32),
             dma((5,)),
             dma,
             dma((n_pair + 1, 2)),
+            dma,
             dma,
             pltpu.SemaphoreType.REGULAR,
         ],
@@ -581,7 +583,7 @@
             2 * cells == LANES * blocks
             and mesh.shape["row"] % 2 == 0
             and mesh.shape["col"] > 1
-            and pairs % 2 == 0
+            and pairs > 2
             and coords.shape[0] == pairs
             and coords.shape[1] + 2 <= PIECES
             and 8 * pairs * cells * cells <= FUSED_BYTES

time: 13.9 us -> 13.6 us (0.978)
  Pallas kernels: 13.1 us -> 12.8 us
    pallas_call x1, Pallas kernels: 12.4 us -> 12.1 us  [per_device_fused(): pl.pallas_call(functools.partial(fused, (n_pair, n_row, n_col, tile)), ou...]
where the time goes in v5:
time: 13.6 us; the launch traced here: 13.4 us
  Pallas kernels  12.8 us (94%)
  between operations  0.64 us (5%)
    pallas_call x1, Pallas kernels, per_device_fused(): pl.pallas_call(functools.partial(fused, (n_pair, n_row, n_col, tile)), ou...  12.1 us
    pallas_call x1, Pallas kernels, per_device_fused(): pl.pallas_call(written, out_shape=(jax.ShapeDtypeStruct(fates.shape, jnp....  0.62 us

profile of v5, /device:TPU:0, one launch (start us, length us, event | category | flops | bytes accessed | tf_op | source)
XLA Modules:
  0.0 13.4 jit_solution(16654081051323612112)
XLA Ops:
  0.6 12.1 %shard_map.68 = (f32[1,16,64]{2,1,0:T(8,128)S(1)}, f32[1,64]{1,0:T(1,128)S(1)}) custom-call(s32[5]{0:T(128)} %counts_in.1, f32[30,1,64]{2,1,0:T(1,128)} %bitcast.2, f32[30,64]{1,0:T(8,128)} %final_in.1, f32[1,64]{1,0:T(1,128)} %growth_in.1, s32[1,64]{1,0:T(1,128)} %bitcast.3), custom_call_target="tpu_custom_call" | custom-call | tf_op jit(solution)/shard_map/pallas_call | solution.py:526
  12.8 0.6 %shard_map.69 = (f32[1,16,64]{2,1,0:T(8,128)}, f32[1,64]{1,0:T(1,128)}) custom-call(f32[1,16,64]{2,1,0:T(8,128)S(1)} %get-tuple-element.4.fates_ref, f32[1,64]{1,0:T(1,128)S(1)} %get-tuple-element.5.mass_ref), custom_call_target="tpu_custom_call" | custom-call | tf_op jit(solution)/shard_map/pallas_call | solution.py:556

commit v6 on v5

--- a/solution.py
+++ b/solution.py
@@ -307,8 +307,10 @@
         for load in own_loads[:2]:
             load.wait()
         xg[first * n_block] = packed(coords_ref[:, 0, :], growth_ref[...])
-        pl.semaphore_wait(barrier, n_block)
-        for block in [0, *order]:
+        pl.semaphore_wait(barrier, 1)
+        send(first, 0)
+        pl.semaphore_wait(barrier, n_block - 1)
+        for block in order:
             send(first, block)
         arrival(results.at[first], result_recv).wait_recv()
         fates_ref[0] = results[first, :CLASSES, :tile]
@@ -321,15 +323,19 @@
         loads = (*own_loads[: 4 if odd else 2], count_load)
         for load in loads:
             load.start()
-        if odd:
+        def allow():
             for block in (*order, 0):
                 for pair in range(2, n_pair):
                     signal(barrier, pair, block)
+
+        if odd:
+            pl.when(mine == 0)(allow)
         else:
             signal(barrier, 1, mine)
         loop(mine + 1, n_block, functools.partial(signal, barrier, first))
         if odd:
             pl.semaphore_wait(barrier, mine + 1)
+            pl.when(mine > 0)(allow)
         else:
             pl.when(mine > 0)(lambda: pl.semaphore_wait(barrier, mine))
         loop(0, mine, functools.partial(signal, ready, first))

time: 13.6 us -> 13.4 us (0.985)
  Pallas kernels: 12.8 us -> 12.6 us
    pallas_call x1, Pallas kernels: 12.1 us -> 11.9 us  [per_device_fused(): pl.pallas_call(functools.partial(fused, (n_pair, n_row, n_col, tile)), ou...]
where the time goes in v6:
time: 13.4 us; the launch traced here: 13.2 us
  Pallas kernels  12.6 us (94%)
  between operations  0.64 us (5%)
    pallas_call x1, Pallas kernels, per_device_fused(): pl.pallas_call(functools.partial(fused, (n_pair, n_row, n_col, tile)), ou...  11.9 us
    pallas_call x1, Pallas kernels, per_device_fused(): pl.pallas_call(written, out_shape=(jax.ShapeDtypeStruct(fates.shape, jnp....  0.62 us

profile of v6, /device:TPU:0, one launch (start us, length us, event | category | flops | bytes accessed | tf_op | source)
XLA Modules:
  0.0 13.2 jit_solution(12489722331289065201)
XLA Ops:
  0.6 11.9 %shard_map.68 = (f32[1,16,64]{2,1,0:T(8,128)S(1)}, f32[1,64]{1,0:T(1,128)S(1)}) custom-call(s32[5]{0:T(128)} %counts_in.1, f32[30,1,64]{2,1,0:T(1,128)} %bitcast.2, f32[30,64]{1,0:T(8,128)} %final_in.1, f32[1,64]{1,0:T(1,128)} %growth_in.1, s32[1,64]{1,0:T(1,128)} %bitcast.3), custom_call_target="tpu_custom_call" | custom-call | tf_op jit(solution)/shard_map/pallas_call | solution.py:532
  12.6 0.6 %shard_map.69 = (f32[1,16,64]{2,1,0:T(8,128)}, f32[1,64]{1,0:T(1,128)}) custom-call(f32[1,16,64]{2,1,0:T(8,128)S(1)} %get-tuple-element.4.fates_ref, f32[1,64]{1,0:T(1,128)S(1)} %get-tuple-element.5.mass_ref), custom_call_target="tpu_custom_call" | custom-call | tf_op jit(solution)/shard_map/pallas_call | solution.py:562

commit v7 on v6

--- a/solution.py
+++ b/solution.py
@@ -124,7 +124,7 @@
 PIECES = 32
 HALF = 16
 BIG = 1e30
-LOG2E = 1.4426950408889634
+SCALE = 1.6986436005760381
 MESH = pl.DeviceIdType.MESH
 
 
@@ -224,13 +224,16 @@
 
         lax.fori_loop(start, stop, step, 0)
 
-    count_load = pltpu.make_async_copy(counts_in, counts_ref, own_sems.at[4])
+    count_load = pltpu.make_async_copy(counts_in, counts_ref, own_sems.at[2])
     own_loads = (
         pltpu.make_async_copy(coords_in, coords_ref, own_sems.at[0]),
         pltpu.make_async_copy(growth_in, growth_ref, own_sems.at[1]),
-        pltpu.make_async_copy(final_in, final_ref, own_sems.at[2]),
-        pltpu.make_async_copy(labels_in, labels_ref, own_sems.at[3]),
-    )
+        pltpu.make_async_copy(final_in, final_ref, f_recv),
+        pltpu.make_async_copy(labels_in, labels_ref, result_recv),
+    )
+    for load in own_loads[:2]:
+        load.start()
+
     def block_copy(time, pair, block):
         row, col = at(block)
         there = (col_at - col) % n_col * n_row + (row_at - row) % n_row
@@ -238,7 +241,7 @@
             src_ref=xg.at[time * n_block],
             dst_ref=xg.at[time * n_block + there],
             send_sem=x_send,
-            recv_sem=x_recv.at[time, there // near],
+            recv_sem=x_recv.at[time - pair, there // near],
             device_id=(pair, row, col),
             device_id_type=MESH,
         )
@@ -302,8 +305,6 @@
         )
 
     def only_send(first):
-        for load in own_loads[:2]:
-            load.start()
         for load in own_loads[:2]:
             load.wait()
         xg[first * n_block] = packed(coords_ref[:, 0, :], growth_ref[...])
@@ -321,7 +322,7 @@
         odd = first == 1
         stop = n_pair if odd else 2
         loads = (*own_loads[: 4 if odd else 2], count_load)
-        for load in loads:
+        for load in loads[2:]:
             load.start()
         def allow():
             for block in (*order, 0):
@@ -368,7 +369,7 @@
                 start, end = parts[part]
                 if part == 0 and (time == first or (odd and time == n_pair)):
                     start = 1
-                arrival(blocks(time, start, end - start), x_recv.at[time, part]).wait_recv()
+                arrival(blocks(time, start, end - start), x_recv.at[time - first, part]).wait_recv()
                 if odd and time < first + 2:
                     relay(time, part).start()
 
@@ -380,18 +381,22 @@
             for time in range(first, stop + 1):
                 z = unpacked(xg, time * n_block + start, time * n_block + end)
                 extras[time, part] = z[pca : pca + 1]
-                z = jnp.where(feature < pca, z, 0.0)
-                norm = jnp.sum(z * z, axis=0, keepdims=True) * LOG2E
+                z = jnp.where(feature < pca, z * SCALE, 0.0)
+                norm = jnp.sum(z * z, axis=0, keepdims=True) * 0.5
+                q = jnp.where(feature < pca, z, jnp.where(feature == pca, -norm, 1.0))
+                q1, q2, q3 = split3(q)
                 if time < stop:
-                    a = jnp.where(
-                        feature < pca, z * (2.0 * LOG2E), jnp.where(feature == pca, -norm, 1.0)
-                    )
-                    a1, a2, a3 = split3(a)
-                    rights[time, part] = jnp.concatenate([a1, a2, a1, a2, a3, a1], axis=0)
+                    rights[time, part] = jnp.concatenate([q1, q2, q1, q2, q3, q1], axis=0)
                 if time > first:
                     low = jnp.where(valid[time][:, lanes], -norm, -BIG)
-                    b = jnp.where(feature < pca, z, jnp.where(feature == pca, 1.0, low))
-                    b1, b2, b3 = split3(b)
+                    ends = jnp.where(feature[HALF:] == pca, 1.0, low)
+                    pieces_of = [
+                        jnp.concatenate(
+                            [one[:HALF], jnp.where(feature[HALF:] < pca, one[HALF:], end)], axis=0
+                        )
+                        for one, end in zip((q1, q2, q3), split3(ends), strict=True)
+                    ]
+                    b1, b2, b3 = pieces_of
                     lefts[time, part] = jnp.concatenate([b1, b1, b2, b2, b1, b3], axis=0)
 
         def fill(pair, part, other):
@@ -473,14 +478,25 @@
             fill(pair, 1, 0)
             fill(pair, 1, 1)
         settle(lead)
+        share = {pair: jnp.where(valid[pair], 1.0 / row_totals[pair], 0.0) for pair in lead}
         if odd:
             classes = lax.broadcasted_iota(jnp.int32, (CLASSES, cells), 0).astype(jnp.float32)
             fates = jnp.where((extra(n_pair) == classes) & valid[n_pair], 1.0, 0.0)
         else:
+            turned = jnp.transpose(jnp.broadcast_to(share[1], (8, cells)))[:, :1]
+            near_high, near_low = k1[0, :, :LANES], k2[0, :, :LANES]
+            scaled = (near_high.astype(jnp.float32) + near_low.astype(jnp.float32)) * turned
+            b1, b2 = split2(scaled)
+            both = dot(k1[1], jnp.concatenate([b1, b2], axis=1), ((1,), (0,)))
+            chain = both[:, :LANES] + both[:, LANES:] + dot(k2[1], b1, ((1,), (0,)))
+            h1, h2 = split2(chain)
             f_copy.wait_recv()
-            fates = fin[...]
+            f1, f2 = split2(fin[...])
+            both = dot(jnp.concatenate([f1, f2], axis=0), h1, ((1,), (0,)))
+            both = both[:CLASSES] + both[CLASSES:] + dot(f1, h2, ((1,), (0,)))
+            fates = both * share[0][:, :LANES]
         own = {}
-        for pair in range(stop - 1, first, -1):
+        for pair in lead if odd else ():
             fates = advance(pair, fates)
             own[pair] = fates[:, :LANES]
         if odd:
@@ -494,7 +510,7 @@
                 for other in range(2):
                     fill(first, part, other)
             settle([first])
-        fates = advance(first, fates)
+            fates = advance(first, fates)
         fates_ref[0] = fates[:, :tile]
         mass_ref[...] = moved(first)[:, :tile]
         number = n_block - 1
@@ -550,9 +566,9 @@
             pltpu.VMEM((CLASSES, cells), jnp.float32),
             pltpu.VMEM((CLASSES, cells), jnp.float32),
             pltpu.VMEM((n_pair, CLASSES + 8, LANES), jnp.float32),
-            dma((5,)),
+            dma((3,)),
             dma,
-            dma((n_pair + 1, 2)),
+            dma((n_pair, 2)),
             dma,
             dma,
             pltpu.SemaphoreType.REGULAR,

time: 13.4 us -> 13.3 us (level)
  Pallas kernels: 12.6 us -> 12.4 us
    pallas_call x1, Pallas kernels: 11.9 us -> 11.8 us  [per_device_fused(): pl.pallas_call(functools.partial(fused, (n_pair, n_row, n_col, tile)), ou...]
where the time goes in v7:
time: 13.3 us; the launch traced here: 13 us
  Pallas kernels  12.4 us (93%)
  between operations  0.64 us (5%)
    pallas_call x1, Pallas kernels, per_device_fused(): pl.pallas_call(functools.partial(fused, (n_pair, n_row, n_col, tile)), ou...  11.8 us
    pallas_call x1, Pallas kernels, per_device_fused(): pl.pallas_call(written, out_shape=(jax.ShapeDtypeStruct(fates.shape, jnp....  0.62 us

profile of v7, /device:TPU:0, one launch (start us, length us, event | category | flops | bytes accessed | tf_op | source)
XLA Modules:
  0.0 13.0 jit_solution(4752749760498956277)
XLA Ops:
  0.6 11.8 %shard_map.68 = (f32[1,16,64]{2,1,0:T(8,128)S(1)}, f32[1,64]{1,0:T(1,128)S(1)}) custom-call(s32[5]{0:T(128)} %counts_in.1, f32[30,1,64]{2,1,0:T(1,128)} %bitcast.2, f32[30,64]{1,0:T(8,128)} %final_in.1, f32[1,64]{1,0:T(1,128)} %growth_in.1, s32[1,64]{1,0:T(1,128)} %bitcast.3), custom_call_target="tpu_custom_call" | custom-call | tf_op jit(solution)/shard_map/pallas_call | solution.py:548
  12.4 0.6 %shard_map.69 = (f32[1,16,64]{2,1,0:T(8,128)}, f32[1,64]{1,0:T(1,128)}) custom-call(f32[1,16,64]{2,1,0:T(8,128)S(1)} %get-tuple-element.4.fates_ref, f32[1,64]{1,0:T(1,128)S(1)} %get-tuple-element.5.mass_ref), custom_call_target="tpu_custom_call" | custom-call | tf_op jit(solution)/shard_map/pallas_call | solution.py:578

commit v8 on v7

--- a/solution.py
+++ b/solution.py
@@ -425,10 +425,10 @@
                 share = jnp.sqrt(extra(pair) / numbers[pair])
                 scale_u[pair] = jnp.where(valid[pair], share * lax.rsqrt(total), 0.0)
             sums = {pair: jnp.zeros((8, cells), jnp.float32) for pair in pairs}
-            for slot in range(n_block):
-                rows = slice(slot * tile, (slot + 1) * tile)
-                row, col = place(slot)
-                position = (row * n_col + col) * tile + iota_rows
+            for start in range(0, cells, 32):
+                rows = slice(start, start + 32)
+                row, col = place(start // tile)
+                position = (row * n_col + col) * tile + start % tile + iota_rows[:32]
                 for pair in pairs:
                     values = kernel[pair, rows, :]
                     terms = values * scale_u[pair]
@@ -438,10 +438,10 @@
                     column = jnp.sum(folded, axis=1, keepdims=True)
                     is_target = position < counts_ref[pair + 1]
                     column = jnp.where(is_target, column, 1.0)
-                    power = jnp.log2(column) + jnp.log2(jnp.full((tile, 1), numbers[pair + 1]))
+                    power = jnp.log2(column) + jnp.log2(jnp.full((32, 1), numbers[pair + 1]))
                     scale_v = jnp.where(is_target, jnp.exp2(-target_power * power), 0.0)
                     scaled = values * scale_v
-                    for k in range(tile // 8):
+                    for k in range(32 // 8):
                         sums[pair] = sums[pair] + scaled[k * 8 : (k + 1) * 8]
                     high, low = split2(scaled)
                     k1[pair, rows, :] = high
@@ -490,6 +490,8 @@
             both = dot(k1[1], jnp.concatenate([b1, b2], axis=1), ((1,), (0,)))
             chain = both[:, :LANES] + both[:, LANES:] + dot(k2[1], b1, ((1,), (0,)))
             h1, h2 = split2(chain)
+            mass_ref[...] = moved(0)[:, :tile]
+            arrival(blocks(0, 0, n_block - 1), x_recv.at[0, 0]).wait_send()
             f_copy.wait_recv()
             f1, f2 = split2(fin[...])
             both = dot(jnp.concatenate([f1, f2], axis=0), h1, ((1,), (0,)))
@@ -512,14 +514,13 @@
             settle([first])
             fates = advance(first, fates)
         fates_ref[0] = fates[:, :tile]
-        mass_ref[...] = moved(first)[:, :tile]
-        number = n_block - 1
         if odd:
-            number = 2 * number + 2 * n_block
+            mass_ref[...] = moved(first)[:, :tile]
             f_copy.wait_send()
             for pair in lead:
                 result_copy(pair).wait_send()
-        arrival(blocks(0, 0, number), x_recv.at[0, 0]).wait_send()
+            number = 2 * (n_block - 1) + 2 * n_block
+            arrival(blocks(0, 0, number), x_recv.at[0, 0]).wait_send()
 
     for pair in range(n_pair):
         pl.when(pair_at == pair)(functools.partial(body if pair < 2 else only_send, pair))

time: 13.3 us -> 13.3 us (level)
  no operation moved by 1% of the time
where the time goes in v8:
time: 13.3 us; the launch traced here: 13 us
  Pallas kernels  12.4 us (93%)
  between operations  0.64 us (5%)
    pallas_call x1, Pallas kernels, per_device_fused(): pl.pallas_call(functools.partial(fused, (n_pair, n_row, n_col, tile)), ou...  11.8 us
    pallas_call x1, Pallas kernels, per_device_fused(): pl.pallas_call(written, out_shape=(jax.ShapeDtypeStruct(fates.shape, jnp....  0.62 us

profile of v8, /device:TPU:0, one launch (start us, length us, event | category | flops | bytes accessed | tf_op | source)
XLA Modules:
  0.0 13.0 jit_solution(15850878543029467663)
XLA Ops:
  0.6 11.8 %shard_map.68 = (f32[1,16,64]{2,1,0:T(8,128)S(1)}, f32[1,64]{1,0:T(1,128)S(1)}) custom-call(s32[5]{0:T(128)} %counts_in.1, f32[30,1,64]{2,1,0:T(1,128)} %bitcast.2, f32[30,64]{1,0:T(8,128)} %final_in.1, f32[1,64]{1,0:T(1,128)} %growth_in.1, s32[1,64]{1,0:T(1,128)} %bitcast.3), custom_call_target="tpu_custom_call" | custom-call | tf_op jit(solution)/shard_map/pallas_call | solution.py:549
  12.4 0.6 %shard_map.69 = (f32[1,16,64]{2,1,0:T(8,128)}, f32[1,64]{1,0:T(1,128)}) custom-call(f32[1,16,64]{2,1,0:T(8,128)S(1)} %get-tuple-element.4.fates_ref, f32[1,64]{1,0:T(1,128)S(1)} %get-tuple-element.5.mass_ref), custom_call_target="tpu_custom_call" | custom-call | tf_op jit(solution)/shard_map/pallas_call | solution.py:579
